TPU v7x, 32 devices: a whole 2x2x4 slice. The times are simulated.
32 devices in a mesh: replica: 4 (over y, x), fsdp: 8 (over z, core).
Axes of the slice: x: 2, y: 2, z: 4, core: 2. Of those that a mesh axis runs over, the one named last changes fastest.
Arguments:
- local_weights: bfloat16 [4, 256, 28672], P('replica', 'fsdp'), may hold values from -6 to 6
- base_weights: float32 [256, 28672], P('fsdp'), may hold values from -6 to 6
- momentum: float32 [256, 28672], P('replica', 'fsdp'), may hold values from -4 to 4
Outputs:
- new_weights: float32 [256, 28672], P('fsdp')
- new_momentum: float32 [256, 28672], P('replica', 'fsdp')
All inputs are finite; a program needn't handle non-finite values. Where the computation divides by a largest or mean magnitude, that divisor is 1e-20 or more.
Results may differ from a plain program's by a relative error of at most 0.015.
Values may be sent and summed in bfloat16 or wider, within the bound.
A program may use at most 128 MiB of HBM per device.

v0:
```python
import jax
import jax.numpy as jnp
from jax import lax
from jax.sharding import PartitionSpec as P

QBLOCK = 128
EPSILON = 1e-06
LEARN_RATE = 0.7
MOMENTUM_COEF = 0.9


def dequantise(integer_levels, block_scales):
    shaped = integer_levels.astype(jnp.float32).reshape(block_scales.shape + (QBLOCK,))
    values = shaped * block_scales.astype(jnp.float32)[..., None]
    return values.reshape(integer_levels.shape)


def per_device(local_weights, base_weights, momentum):
    row_count, col_count = base_weights.shape
    replica_differences = base_weights - local_weights[0].astype(jnp.float32)
    block_grouped = replica_differences.reshape(row_count, col_count // QBLOCK, QBLOCK)
    block_scales = (jnp.max(jnp.abs(block_grouped), axis=2) + EPSILON).astype(jnp.bfloat16)
    integer_levels = (block_grouped / block_scales.astype(jnp.float32)[:, :, None]).astype(
        jnp.bfloat16
    )
    levels_local = integer_levels.reshape(1, row_count, col_count)
    scales_local = block_scales.reshape(1, row_count, col_count // QBLOCK)
    replica_count = lax.axis_size("replica")
    shard_group_count = lax.axis_size("fsdp")
    group = shard_group_count // replica_count
    piece = momentum.shape[1] // shard_group_count
    levels_owned, scales_owned = (
        lax.all_to_all(levels_local, "replica", split_axis=2, concat_axis=0, tiled=True),
        lax.all_to_all(scales_local, "replica", split_axis=2, concat_axis=0, tiled=True),
    )
    summed = jnp.sum(dequantise(levels_owned, scales_owned), axis=0)
    sectioned = momentum.reshape(group, row_count, shard_group_count, piece)
    sectioned = lax.all_to_all(sectioned, "fsdp", split_axis=2, concat_axis=2, tiled=True)
    sectioned = lax.all_to_all(sectioned, "replica", split_axis=2, concat_axis=0, tiled=True)
    sectioned = lax.all_to_all(sectioned, "fsdp", split_axis=0, concat_axis=3, tiled=True)
    owned_momentum = sectioned.reshape(row_count, col_count // replica_count)
    average = summed / replica_count
    owned_new = MOMENTUM_COEF * owned_momentum + average
    update = (LEARN_RATE * (average + MOMENTUM_COEF * owned_new)).astype(jnp.bfloat16)
    returned = lax.all_gather(update, "replica", axis=1, tiled=True)
    going = owned_new.reshape(1, row_count, group, shard_group_count * piece)
    going = lax.all_to_all(going, "fsdp", split_axis=3, concat_axis=0, tiled=True)
    going = lax.all_to_all(going, "replica", split_axis=0, concat_axis=2, tiled=True)
    going = lax.all_to_all(going, "fsdp", split_axis=2, concat_axis=2, tiled=True)
    new_momentum = going.reshape(momentum.shape)
    new_weights = base_weights - returned.astype(jnp.float32)
    return (new_weights, new_momentum)


def solution(mesh):
    return jax.shard_map(
        per_device,
        mesh=mesh,
        in_specs=(P("replica", "fsdp", None), P("fsdp", None), P("replica", "fsdp")),
        out_specs=(P("fsdp", None), P("replica", "fsdp")),
        check_vma=False,
    )
```

profile of v0, /device:TPU:0, one launch (start us, length us, event | category | flops | bytes accessed | tf_op | source)
XLA Modules:
  0.0 445.3 jit_solution(15897536443774673228)
XLA Ops:
  7.2 3.0 abs_bitcast_fusion
  10.2 2.5 copy.72
  12.6 3.3 reduce_max.9
  18.3 5.2 %all-to-all-start.1 = ((bf16[4,2,896]{2,1,0:T(2,128)(2,1)}), bf16[4,2,896]{2,1,0:T(2,128)(2,1)S(1)}, u32[]{:S(2)}, u32[]{:S(2)}) async-start(bf16[4,2,896]{2,1,0:T(2,128)(2,1)} %reshape.110), calls=%async_computation.1 | async-start | bytes 28672 | tf_op jit(solution)/shard_map/all_to_all | solution.py:34
  25.5 3.6 fusion.2
  29.1 27.0 %copy.56 = bf16[1,32,28672]{1,0,2:T(2,128)(2,1)} copy(bf16[1,32,28672]{2,1,0:T(8,128)(2,1)} %fusion.2) | data formatting | bytes 3670016 | tf_op jit(solution)/shard_map/convert_element_type | solution.py:23
  56.1 157.0 %reduce.2 = bf16[28672,32]{1,0:T(8,128)(2,1)} reduce(bf16[28672,1,32]{2,1,0:T(2,128)(2,1)} %bitcast.64, bf16[]{:T(256)} %broadcast.56), dimensions={1}, to_apply=%bitcast.56.reduce_sub_computation | reduce | bytes 3670018
  213.2 9.4 %reshape.108 = bf16[4,2,114688]{2,1,0:T(2,128)(2,1)} reshape(bf16[28672,32]{1,0:T(8,128)(2,1)} %reduce.2) | data formatting | bytes 3670016
  222.6 4.3 all-to-all-start
  226.9 1.5 reshape.102
  228.4 1.8 copy.59
  230.2 18.3 %all-to-all-done = bf16[4,2,114688]{2,1,0:T(2,128)(2,1)S(1)} async-done(((bf16[4,2,114688]{2,1,0:T(2,128)(2,1)}), bf16[4,2,114688]{2,1,0:T(2,128)(2,1)S(1)}, u32[]{:S(2)}, u32[]{:S(2)}) %all-to-all-start) | async-done | bytes 1835040 | tf_op jit(solution)/shard_map/all_to_all | solution.py:33
  248.5 31.3 %all_to_all.91 = f32[2,32,8,448]{3,1,0,2:T(8,128)} all-to-all(f32[2,32,8,448]{3,1,0,2:T(8,128)S(1)} %copy.59), channel_id=1, replica_groups=mesh['replica'=4,'fsdp'=8] {'fsdp'}, dimensions={2} | all-to-all | bytes 1835008 | tf_op jit(solution)/shard_map/all_to_all | solution.py:38
  279.9 3.5 all-to-all-start.3
  283.6 8.1 %reshape.109 = bf16[28672,1,32]{2,1,0:T(2,128)(2,1)} reshape(bf16[4,2,114688]{2,1,0:T(2,128)(2,1)S(1)} %all-to-all-done) | data formatting | bytes 3670016
  291.8 5.1 %all-to-all-done.3 = f32[2,32,8,448]{3,1,0,2:T(8,128)S(1)} async-done(((f32[2,32,8,448]{3,1,0,2:T(8,128)}), f32[2,32,8,448]{3,1,0,2:T(8,128)S(1)}, u32[]{:S(2)}, u32[]{:S(2)}) %all-to-all-start.3) | async-done | bytes 917536 | tf_op jit(solution)/shard_map/all_to_all | solution.py:39
  296.9 1.8 copy.60
  298.8 3.6 all-to-all-start.4
  302.4 17.6 %bitcast_convert_fusion = f32[1,32,28672]{1,0,2:T(1,128)} fusion(bf16[28672,1,32]{2,1,0:T(2,128)(2,1)} %reshape.109), kind=kLoop, calls=%fused_computation.15 | loop fusion | flops 917504 | bytes 5505024 | tf_op jit(solution)/shard_map/convert_element_type | solution.py:13
  319.9 8.9 %fusion = f32[32,7168]{0,1:T(8,128)} fusion(f32[4,1,32,7168]{2,3,0,1:T(8,128)} %bitcast.65, f32[4,32,56]{1,2,0:T(8,128)S(1)} %bitcast.76), kind=kLoop, calls=%fused_computation.1 | loop fusion | flops 1605632 | bytes 4616192 | tf_op jit(solution)/shard_map/reduce_sum | solution.py:36
  328.8 3.3 copy.58
  334.4 2.2 broadcast_multiply_fusion
  338.0 3.6 copy.64
  341.6 5.2 %reshape.112 = f32[8,1,28672]{2,1,0:T(1,128)S(1)} reshape(f32[3584,1,2,32]{3,2,1,0:T(2,128)} %bitcast.67) | data formatting | bytes 1835008
  346.8 28.5 %all_to_all.92 = f32[8,1,28672]{2,1,0:T(1,128)S(1)} all-to-all(f32[8,1,28672]{2,1,0:T(1,128)S(1)} %reshape.112), channel_id=1, replica_groups=mesh['replica'=4,'fsdp'=8] {'fsdp'}, dimensions={0} | all-to-all | bytes 1835008 | tf_op jit(solution)/shard_map/all_to_all | solution.py:47
  375.8 2.8 reduce.4
  378.6 4.9 %reshape.113 = f32[3584,1,2,32]{3,2,1,0:T(2,128)} reshape(f32[8,28672]{1,0:T(8,128)S(1)} %reduce.4) | data formatting | bytes 1835008
  383.6 5.0 %copy.71 = f32[1,32,2,8,448]{4,1,2,3,0:T(8,128)S(1)} copy(f32[1,32,2,8,448]{1,2,4,3,0:T(2,128)} %bitcast.68) | data formatting | bytes 1835008 | tf_op jit(solution)/shard_map/all_to_all | solution.py:47
  388.6 16.7 %all_to_all.93 = f32[8,32,2,448]{3,1,2,0:T(8,128)S(1)} all-to-all(f32[8,32,2,448]{3,1,2,0:T(8,128)S(1)} %bitcast.74), channel_id=1, replica_groups=mesh['replica'=4,'fsdp'=8] {'replica'}, dimensions={0} | all-to-all | bytes 1835008 | tf_op jit(solution)/shard_map/all_to_all | solution.py:48
  406.4 3.6 all-to-all-start.7
  410.0 4.8 %convert_subtract_fusion.1 = f32[32,28672]{1,0:T(8,128)} fusion(f32[32,28672]{1,0:T(8,128)} %param.4, bf16[32,28672]{1,0:T(8,128)(2,1)} %all-gather.2.cloned.1.call-done), kind=kLoop, calls=%fused_computation.5 | loop fusion | flops 1835008 | bytes 9175040 | tf_op jit(solution)/shard_map/sub | solution.py:51
  414.8 21.7 %all-to-all-done.7 = f32[2,32,8,448]{3,1,0,2:T(8,128)S(1)} async-done(((f32[2,32,8,448]{3,1,0,2:T(8,128)}), f32[2,32,8,448]{3,1,0,2:T(8,128)S(1)}, u32[]{:S(2)}, u32[]{:S(2)}) %all-to-all-start.7) | async-done | bytes 917536 | tf_op jit(solution)/shard_map/all_to_all | solution.py:49
  (31 shorter events, 11.9 us)
Async XLA Ops:
  12.6 11.9 %copy-start.1 = (bf16[1,32,28672]{2,1,0:T(8,128)(2,1)S(1)}, bf16[1,32,28672]{2,1,0:T(8,128)(2,1)}, u32[]{:S(2)}) copy-start(bf16[1,32,28672]{2,1,0:T(8,128)(2,1)} %param.3) | copy-start | bytes 5505028
  18.3 204.3 %all-to-all-start.1 = ((bf16[4,2,896]{2,1,0:T(2,128)(2,1)}), bf16[4,2,896]{2,1,0:T(2,128)(2,1)S(1)}, u32[]{:S(2)}, u32[]{:S(2)}) async-start(bf16[4,2,896]{2,1,0:T(2,128)(2,1)} %reshape.110), calls=%async_computation.1 | async-start | bytes 28672 | tf_op jit(solution)/shard_map/all_to_all | solution.py:34
  23.5 2.0 copy-start
  222.6 4.3 copy-start.2
  222.6 26.0 %all-to-all-start = ((bf16[4,2,114688]{2,1,0:T(2,128)(2,1)}), bf16[4,2,114688]{2,1,0:T(2,128)(2,1)S(1)}, u32[]{:S(2)}, u32[]{:S(2)}) async-start(bf16[4,2,114688]{2,1,0:T(2,128)(2,1)} %reshape.108), calls=%async_computation | async-start | bytes 3670016 | tf_op jit(solution)/shard_map/all_to_all | solution.py:33
  279.9 17.0 %all-to-all-start.3 = ((f32[2,32,8,448]{3,1,0,2:T(8,128)}), f32[2,32,8,448]{3,1,0,2:T(8,128)S(1)}, u32[]{:S(2)}, u32[]{:S(2)}) async-start(f32[2,32,8,448]{3,1,0,2:T(8,128)} %all_to_all.91), calls=%async_computation.3 | async-start | bytes 2097152 | tf_op jit(solution)/shard_map/all_to_all | solution.py:39
  298.8 33.4 %all-to-all-start.4 = ((f32[8,32,2,448]{3,2,1,0:T(2,128)}), f32[8,32,2,448]{3,2,1,0:T(2,128)S(1)}, u32[]{:S(2)}, u32[]{:S(2)}) async-start(f32[8,32,2,448]{3,2,1,0:T(2,128)} %bitcast.71), calls=%async_computation.4 | async-start | bytes 2097152 | tf_op jit(solution)/shard_map/all_to_all | solution.py:40
  302.3 107.7 %all-gather.2.cloned.1.call-start = ((), (), s32[]{:S(2)}) async-start(), calls=%async_computation.8 | async-start | bytes 2293760 | tf_op jit(solution)/shard_map/all_gather | solution.py:45
  406.4 30.1 %all-to-all-start.7 = ((f32[2,32,8,448]{3,1,0,2:T(8,128)}), f32[2,32,8,448]{3,1,0,2:T(8,128)S(1)}, u32[]{:S(2)}, u32[]{:S(2)}) async-start(f32[2,32,8,448]{3,1,0,2:T(8,128)} %copy.68), calls=%async_computation.7 | async-start | bytes 2097152 | tf_op jit(solution)/shard_map/all_to_all | solution.py:49
Sparse Core Ops, SparseCore 0:
  337.9 33.3 all-gather.1
where the time goes:
time: 449 us; the launch traced here: 445 us
  other arithmetic  205 us (46%)
  local copies, waits for them, and re-layouts  84.3 us (19%)
  blocking collectives  76.5 us (17%)
  waiting for transfers between devices  45.2 us (10%)
  starting transfers between devices  20.2 us (4%)
  between operations  14.2 us (3%)
    unnamed x3, other arithmetic  161 us
    unnamed x14, local copies, waits for them, and re-layouts  32.5 us
    all_to_all x1, blocking collectives, per_device(): lax.all_to_all(sectioned, 'fsdp', split_axis=2, concat_axis=2, tiled=True)  31.3 us
    all_to_all x1, blocking collectives, per_device(): lax.all_to_all(going, 'fsdp', split_axis=3, concat_axis=0, tiled=True)  28.5 us
    convert_element_type x1, local copies, waits for them, and re-layouts, per_device(): (block_grouped / block_scales.astype(jnp.float32)[:, :, None]).astype(jnp...  27 us
    all_to_all x1, waiting for transfers between devices, per_device(): lax.all_to_all(going, 'fsdp', split_axis=2, concat_axis=2, tiled=True)  21.7 us
    all_to_all x1, waiting for transfers between devices, per_device(): lax.all_to_all(levels_local, 'replica', split_axis=2, concat_axis=0, tile...  18.3 us
    convert_element_type x1, other arithmetic, dequantise(): integer_levels.astype(jnp.float32).reshape(block_scales.shape + (QBLOCK,))  17.6 us
  transfers between devices with their start and end apart: 6, of which 3 were waited for; matrix products, arithmetic and copies ran while one was open for 60% of the time, Pallas kernels for 0%

commit v1 on v0

--- a/solution.py
+++ b/solution.py
@@ -1,3 +1,4 @@
+import functools
 import jax
 import jax.numpy as jnp
 from jax import lax
@@ -7,6 +8,19 @@
 EPSILON = 1e-06
 LEARN_RATE = 0.7
 MOMENTUM_COEF = 0.9
+
+
+def handle_area(obj, a_name):
+    state_next = lax.all_to_all(
+        jnp.stack(jnp.split(obj, lax.axis_size(a_name), 2), axis=0),
+        axis_name=a_name,
+        split_axis=0,
+        concat_axis=0,
+    )
+    return jnp.concatenate(state_next, 0)
+
+
+panels_work = functools.partial(handle_area, a_name="replica")
 
 
 def dequantise(integer_levels, block_scales):
@@ -30,7 +44,7 @@
     group = shard_group_count // replica_count
     piece = momentum.shape[1] // shard_group_count
     levels_owned, scales_owned = (
-        lax.all_to_all(levels_local, "replica", split_axis=2, concat_axis=0, tiled=True),
+        panels_work(levels_local),
         lax.all_to_all(scales_local, "replica", split_axis=2, concat_axis=0, tiled=True),
     )
     summed = jnp.sum(dequantise(levels_owned, scales_owned), axis=0)

time: 449 us -> 250 us (0.56)
  other arithmetic: 205 us -> 27.7 us
  waiting for transfers between devices: 45.2 us -> 92.8 us
  local copies, waits for them, and re-layouts: 84.3 us -> 45.8 us
  blocking collectives: 76.5 us -> 42.8 us
  starting transfers between devices: 20.2 us -> 25.2 us
    unnamed x3 -> x2, other arithmetic: 161 us -> 3.97 us
    all_to_all x1 -> x0, blocking collectives: 31.3 us -> none  [per_device(): lax.all_to_all(sectioned, 'fsdp', split_axis=2, concat_axis=2, tiled=True)]
    all_to_all x1 -> x2, waiting for transfers between devices: 18.3 us -> 45.3 us  [the longest x1 25.6 us: per_device(): lax.all_to_all(sectioned, 'fsdp', split_axis=2, concat_axis=2, tiled=True)]
    convert_element_type x1 -> x2, local copies, waits for them, and re-layouts: 27 us -> 0.12 us  [dequantise(): values = shaped * block_scales.astype(jnp.float32)[..., None]]
    convert_element_type x3 -> x1, other arithmetic: 17.7 us -> 0.01 us  [per_device(): block_scales.astype(jnp.float32)[:, :, None]]
    unnamed x14 -> x10, local copies, waits for them, and re-layouts: 32.5 us -> 15.1 us
    all_to_all x1, waiting for transfers between devices: 0.01 us -> 15.2 us  [per_device(): lax.all_to_all(sectioned, 'fsdp', split_axis=0, concat_axis=3, tiled=True)]
    mul x0 -> x2, local copies, waits for them, and re-layouts: none -> 7.23 us  [dequantise(): values = shaped * block_scales.astype(jnp.float32)[..., None]]
  transfers between devices with their start and end apart: 6 -> 7, of which waited for: 3 -> 5; matrix products, arithmetic and copies ran while one was open for 60% -> 21% of each run, Pallas kernels for 0% -> 0%
where the time goes in v1:
time: 250 us; the launch traced here: 249 us
  waiting for transfers between devices  92.8 us (37%)
  local copies, waits for them, and re-layouts  45.8 us (18%)
  blocking collectives  42.8 us (17%)
  other arithmetic  27.7 us (11%)
  starting transfers between devices  25.2 us (10%)
  between operations  14.2 us (6%)
    all_to_all x1, blocking collectives, per_device(): lax.all_to_all(going, 'fsdp', split_axis=3, concat_axis=0, tiled=True)  26.2 us
    all_to_all x1, waiting for transfers between devices, per_device(): lax.all_to_all(sectioned, 'fsdp', split_axis=2, concat_axis=2, tiled=True)  25.6 us
    all_to_all x1, waiting for transfers between devices, per_device(): lax.all_to_all(going, 'fsdp', split_axis=2, concat_axis=2, tiled=True)  21.7 us
    all_to_all x1, waiting for transfers between devices, handle_area(): lax.all_to_all(jnp.stack(jnp.split(obj, lax.axis_size(a_name), 2), axis=0...  19.7 us
    all_to_all x1, blocking collectives, per_device(): lax.all_to_all(going, 'replica', split_axis=0, concat_axis=2, tiled=True)  16.7 us
    all_to_all x1, waiting for transfers between devices, per_device(): lax.all_to_all(sectioned, 'fsdp', split_axis=0, concat_axis=3, tiled=True)  15.2 us
    unnamed x10, local copies, waits for them, and re-layouts  15.1 us
    all_to_all x1, waiting for transfers between devices, per_device(): lax.all_to_all(sectioned, 'replica', split_axis=2, concat_axis=0, tiled=T...  10.6 us
  transfers between devices with their start and end apart: 7, of which 5 were waited for; matrix products, arithmetic and copies ran while one was open for 21% of the time, Pallas kernels for 0%

profile of v1, /device:TPU:0, one launch (start us, length us, event | category | flops | bytes accessed | tf_op | source)
XLA Modules:
  0.0 248.5 jit_solution(6518958844856643947)
XLA Ops:
  7.2 3.0 %abs_bitcast_fusion = f32[4,8,224,128]{3,1,2,0:T(8,128)S(1)} fusion(f32[32,28672]{1,0:T(8,128)} %param.4, bf16[1,32,28672]{2,1,0:T(8,128)(2,1)} %param.3), kind=kLoop, calls=%fused_computation.5 | loop fusion | flops 2752512 | bytes 9175040
  10.2 2.5 %copy.60 = f32[4,8,224,128]{3,2,1,0:T(8,128)} copy(f32[4,8,224,128]{3,1,2,0:T(8,128)S(1)} %abs_bitcast_fusion) | data formatting | bytes 7340032
  12.6 3.2 %reduce_max.9 = f32[32,224]{1,0:T(8,128)S(1)} reduce(f32[32,224,128]{2,1,0:T(8,128)} %bitcast.61, f32[]{:T(128)} %constant.1.clone.1), dimensions={2}, to_apply=%region_0.0 | reduce | flops 910336 | bytes 3698692 | tf_op jit(solution)/shard_map/reduce_max | solution.py:36
  18.2 5.2 %all-to-all-start.1 = ((bf16[4,2,896]{2,1,0:T(2,128)(2,1)}), bf16[4,2,896]{2,1,0:T(2,128)(2,1)S(1)}, u32[]{:S(2)}, u32[]{:S(2)}) async-start(bf16[4,2,896]{2,1,0:T(2,128)(2,1)} %reshape.106), calls=%async_computation.1 | async-start | bytes 28672 | tf_op jit(solution)/shard_map/all_to_all | solution.py:48
  25.4 3.8 %fusion.1 = bf16[1,32,28672]{2,1,0:T(8,128)(2,1)S(1)} fusion(f32[4,8,224,128]{3,2,1,0:T(8,128)S(1)} %bitcast.64, f32[32,28672]{1,0:T(8,128)S(1)} %copy-done, bf16[1,32,28672]{2,1,0:T(8,128)(2,1)} %param.3), kind=kLoop, calls=%fused_computation.7 | loop fusion | flops 3670016 | bytes 11010048 | tf_op jit(solution)/shard_map/convert_element_type | solution.py:37
  29.3 1.7 reshape.101
  30.9 1.6 copy.47
  32.5 4.9 %all-to-all-start.2 = ((f32[2,32,8,448]{3,1,0,2:T(8,128)}), f32[2,32,8,448]{3,1,0,2:T(8,128)}, u32[]{:S(2)}, u32[]{:S(2)}) async-start(f32[2,32,8,448]{3,1,0,2:T(8,128)} %copy.47), calls=%async_computation.2 | async-start | bytes 2097152 | tf_op jit(solution)/shard_map/all_to_all | solution.py:52
  38.5 25.6 %all-to-all-done.2 = f32[2,32,8,448]{3,1,0,2:T(8,128)} async-done(((f32[2,32,8,448]{3,1,0,2:T(8,128)}), f32[2,32,8,448]{3,1,0,2:T(8,128)}, u32[]{:S(2)}, u32[]{:S(2)}) %all-to-all-start.2) | async-done | bytes 917536 | tf_op jit(solution)/shard_map/all_to_all | solution.py:52
  64.1 4.2 %all-to-all-start.3 = ((f32[2,32,8,448]{3,1,0,2:T(8,128)}), f32[2,32,8,448]{3,1,0,2:T(8,128)S(1)}, u32[]{:S(2)}, u32[]{:S(2)}) async-start(f32[2,32,8,448]{3,1,0,2:T(8,128)} %all-to-all-done.2), calls=%async_computation.3 | async-start | bytes 2097152 | tf_op jit(solution)/shard_map/all_to_all | solution.py:53
  68.3 2.8 %pad_maximum_fusion = bf16[4,1,32,7168]{3,2,1,0:T(8,128)(2,1)} fusion(bf16[1,1,32,7168]{3,2,1,0:T(8,128)(2,1)} %get-tuple-element.3, bf16[1,1,32,7168]{3,2,1,0:T(8,128)(2,1)} %get-tuple-element.4, bf16[1,1,32,7168]{3,2,1,0:T(8,128)(2,1)} %get-tuple-element.5, bf16[1,1,32,7168]{3,2,1,0:T(8,128)(2,1)S(1)} %get-tuple-element.2), kind=kLoop, calls=%fused_computation.6 | loop fusion | flops 2752512 | bytes 3670016 | tf_op jit(solution)/shard_map/stack | solution.py:15
  71.0 10.6 %all-to-all-done.3 = f32[2,32,8,448]{3,1,0,2:T(8,128)S(1)} async-done(((f32[2,32,8,448]{3,1,0,2:T(8,128)}), f32[2,32,8,448]{3,1,0,2:T(8,128)S(1)}, u32[]{:S(2)}, u32[]{:S(2)}) %all-to-all-start.3) | async-done | bytes 917536 | tf_op jit(solution)/shard_map/all_to_all | solution.py:53
  81.6 3.6 %all-to-all-start = ((bf16[4,1,32,7168]{3,2,1,0:T(8,128)(2,1)}), bf16[4,1,32,7168]{3,2,1,0:T(8,128)(2,1)S(1)}, u32[]{:S(2)}, u32[]{:S(2)}) async-start(bf16[4,1,32,7168]{3,2,1,0:T(8,128)(2,1)} %pad_maximum_fusion), calls=%async_computation | async-start | bytes 3670016 | tf_op jit(solution)/shard_map/all_to_all | solution.py:14
  85.2 1.8 copy.48
  87.0 19.7 %all-to-all-done = bf16[4,1,32,7168]{3,2,1,0:T(8,128)(2,1)S(1)} async-done(((bf16[4,1,32,7168]{3,2,1,0:T(8,128)(2,1)}), bf16[4,1,32,7168]{3,2,1,0:T(8,128)(2,1)S(1)}, u32[]{:S(2)}, u32[]{:S(2)}) %all-to-all-start) | async-done | bytes 1835040 | tf_op jit(solution)/shard_map/all_to_all | solution.py:14
  106.8 3.6 %all-to-all-start.4 = ((f32[8,32,2,448]{3,2,1,0:T(2,128)}), f32[8,32,2,448]{3,2,1,0:T(2,128)S(1)}, u32[]{:S(2)}, u32[]{:S(2)}) async-start(f32[8,32,2,448]{3,2,1,0:T(2,128)} %bitcast.11), calls=%async_computation.4 | async-start | bytes 2097152 | tf_op jit(solution)/shard_map/all_to_all | solution.py:54
  110.9 2.4 mul.46
  113.3 4.8 %mul.47 = f32[4,1,32,7168]{3,2,1,0:T(8,128)} reshape(f32[4,32,56,128]{3,2,1,0:T(8,128)} %mul.46) | data formatting | bytes 7340032 | tf_op jit(solution)/shard_map/mul | solution.py:28
  118.1 3.5 %multiply_reduce_fusion = f32[32,7168]{1,0:T(8,128)} fusion(f32[4,1,32,7168]{3,2,1,0:T(8,128)} %mul.47, bf16[4,1,32,7168]{3,2,1,0:T(8,128)(2,1)S(1)} %all-to-all-done), kind=kLoop, calls=%fused_computation.4 | loop fusion | flops 2523136 | bytes 6422528 | tf_op jit(solution)/shard_map/reduce_sum | solution.py:50
  121.6 15.2 %all-to-all-done.4 = f32[8,32,2,448]{3,2,1,0:T(2,128)S(1)} async-done(((f32[8,32,2,448]{3,2,1,0:T(2,128)}), f32[8,32,2,448]{3,2,1,0:T(2,128)S(1)}, u32[]{:S(2)}, u32[]{:S(2)}) %all-to-all-start.4) | async-done | bytes 917536 | tf_op jit(solution)/shard_map/all_to_all | solution.py:54
  138.6 1.3 mul.52
  139.9 2.1 broadcast_multiply_fusion
  143.5 3.6 %copy.52 = f32[1,32,2,3584]{1,2,0,3:T(2,128)} copy(f32[1,32,2,3584]{3,1,2,0:T(8,128)S(1)} %copy_add_fusion) | data formatting | bytes 1835008 | tf_op jit(solution)/shard_map/add | solution.py:57
  147.1 5.3 %reshape.108 = f32[8,1,28672]{2,1,0:T(1,128)S(1)} reshape(f32[3584,1,2,32]{3,2,1,0:T(2,128)} %bitcast.62) | data formatting | bytes 1835008
  152.4 26.2 %all_to_all.87 = f32[8,1,28672]{2,1,0:T(1,128)S(1)} all-to-all(f32[8,1,28672]{2,1,0:T(1,128)S(1)} %reshape.108), channel_id=1, replica_groups=mesh['replica'=4,'fsdp'=8] {'fsdp'}, dimensions={0} | all-to-all | bytes 1835008 | tf_op jit(solution)/shard_map/all_to_all | solution.py:61
  179.0 2.8 %reduce.3 = f32[8,28672]{1,0:T(8,128)S(1)} reduce(f32[8,1,28672]{2,1,0:T(1,128)S(1)} %all_to_all.87, f32[]{:T(128)} %broadcast.57), dimensions={1}, to_apply=%all_to_all.70.reduce_sub_computation | reduce | bytes 1835012 | tf_op jit(solution)/shard_map/all_to_all | solution.py:61
  181.9 4.9 %reshape.109 = f32[3584,1,2,32]{3,2,1,0:T(2,128)} reshape(f32[8,28672]{1,0:T(8,128)S(1)} %reduce.3) | data formatting | bytes 1835008
  186.8 5.0 %copy.59 = f32[1,32,2,8,448]{4,1,2,3,0:T(8,128)S(1)} copy(f32[1,32,2,8,448]{1,2,4,3,0:T(2,128)} %bitcast.63) | data formatting | bytes 1835008 | tf_op jit(solution)/shard_map/all_to_all | solution.py:61
  191.8 16.7 %all_to_all.88 = f32[8,32,2,448]{3,1,2,0:T(8,128)S(1)} all-to-all(f32[8,32,2,448]{3,1,2,0:T(8,128)S(1)} %bitcast.68), channel_id=1, replica_groups=mesh['replica'=4,'fsdp'=8] {'replica'}, dimensions={0} | all-to-all | bytes 1835008 | tf_op jit(solution)/shard_map/all_to_all | solution.py:62
  209.7 3.6 %all-to-all-start.7 = ((f32[2,32,8,448]{3,1,0,2:T(8,128)}), f32[2,32,8,448]{3,1,0,2:T(8,128)S(1)}, u32[]{:S(2)}, u32[]{:S(2)}) async-start(f32[2,32,8,448]{3,1,0,2:T(8,128)} %copy.56), calls=%async_computation.7 | async-start | bytes 2097152 | tf_op jit(solution)/shard_map/all_to_all | solution.py:63
  213.3 4.8 %convert_subtract_fusion.1 = f32[32,28672]{1,0:T(8,128)} fusion(f32[32,28672]{1,0:T(8,128)} %param.4, bf16[32,28672]{1,0:T(8,128)(2,1)} %all-gather.2.cloned.1.call-done), kind=kLoop, calls=%fused_computation.3 | loop fusion | flops 1835008 | bytes 9175040 | tf_op jit(solution)/shard_map/sub | solution.py:65
  218.0 21.7 %all-to-all-done.7 = f32[2,32,8,448]{3,1,0,2:T(8,128)S(1)} async-done(((f32[2,32,8,448]{3,1,0,2:T(8,128)}), f32[2,32,8,448]{3,1,0,2:T(8,128)S(1)}, u32[]{:S(2)}, u32[]{:S(2)}) %all-to-all-start.7) | async-done | bytes 917536 | tf_op jit(solution)/shard_map/all_to_all | solution.py:63
  (30 shorter events, 12.8 us)
Async XLA Ops:
  18.2 14.3 %all-to-all-start.1 = ((bf16[4,2,896]{2,1,0:T(2,128)(2,1)}), bf16[4,2,896]{2,1,0:T(2,128)(2,1)S(1)}, u32[]{:S(2)}, u32[]{:S(2)}) async-start(bf16[4,2,896]{2,1,0:T(2,128)(2,1)} %reshape.106), calls=%async_computation.1 | async-start | bytes 28672 | tf_op jit(solution)/shard_map/all_to_all | solution.py:48
  23.4 2.0 copy-start
  32.5 31.5 %all-to-all-start.2 = ((f32[2,32,8,448]{3,1,0,2:T(8,128)}), f32[2,32,8,448]{3,1,0,2:T(8,128)}, u32[]{:S(2)}, u32[]{:S(2)}) async-start(f32[2,32,8,448]{3,1,0,2:T(8,128)} %copy.47), calls=%async_computation.2 | async-start | bytes 2097152 | tf_op jit(solution)/shard_map/all_to_all | solution.py:52
  64.1 17.5 %all-to-all-start.3 = ((f32[2,32,8,448]{3,1,0,2:T(8,128)}), f32[2,32,8,448]{3,1,0,2:T(8,128)S(1)}, u32[]{:S(2)}, u32[]{:S(2)}) async-start(f32[2,32,8,448]{3,1,0,2:T(8,128)} %all-to-all-done.2), calls=%async_computation.3 | async-start | bytes 2097152 | tf_op jit(solution)/shard_map/all_to_all | solution.py:53
  81.6 25.1 %all-to-all-start = ((bf16[4,1,32,7168]{3,2,1,0:T(8,128)(2,1)}), bf16[4,1,32,7168]{3,2,1,0:T(8,128)(2,1)S(1)}, u32[]{:S(2)}, u32[]{:S(2)}) async-start(bf16[4,1,32,7168]{3,2,1,0:T(8,128)(2,1)} %pad_maximum_fusion), calls=%async_computation | async-start | bytes 3670016 | tf_op jit(solution)/shard_map/all_to_all | solution.py:14
  106.8 30.1 %all-to-all-start.4 = ((f32[8,32,2,448]{3,2,1,0:T(2,128)}), f32[8,32,2,448]{3,2,1,0:T(2,128)S(1)}, u32[]{:S(2)}, u32[]{:S(2)}) async-start(f32[8,32,2,448]{3,2,1,0:T(2,128)} %bitcast.11), calls=%async_computation.4 | async-start | bytes 2097152 | tf_op jit(solution)/shard_map/all_to_all | solution.py:54
  110.3 102.9 %all-gather.2.cloned.1.call-start = ((), (), s32[]{:S(2)}) async-start(), calls=%async_computation.8 | async-start | bytes 2293760 | tf_op jit(solution)/shard_map/all_gather | solution.py:59
  137.4 2.6 %copy-start.1 = (f32[32,7168]{1,0:T(8,128)S(1)}, f32[32,7168]{1,0:T(8,128)}, u32[]{:S(2)}) copy-start(f32[32,7168]{1,0:T(8,128)} %multiply_reduce_fusion) | copy-start | bytes 2752516
  209.7 30.1 %all-to-all-start.7 = ((f32[2,32,8,448]{3,1,0,2:T(8,128)}), f32[2,32,8,448]{3,1,0,2:T(8,128)S(1)}, u32[]{:S(2)}, u32[]{:S(2)}) async-start(f32[2,32,8,448]{3,1,0,2:T(8,128)} %copy.56), calls=%async_computation.7 | async-start | bytes 2097152 | tf_op jit(solution)/shard_map/all_to_all | solution.py:63
Sparse Core Ops, SparseCore 0:
  143.4 30.9 all-gather.1
